TPU v7x, 128 devices: a whole 4x4x4 slice. The times are simulated.
128 devices in a mesh: gy: 8 (over x_hi, y), gx: 16 (over z, x_lo, core).
Axes of the slice: x: 4 (x_hi: 2, x_lo: 2; x = x_hi * 2 + x_lo), y: 4, z: 4, core: 2. Of those that a mesh axis runs over, the one named last changes fastest.
Arguments:
- features: bfloat16 [256, 2048, 256], P('gy', 'gx'), may hold values from -8 to 8
- tissue: int32 [16, 128], P('gy', 'gx'), may hold values 0 or 1
- owner_map: int32 [8, 16, 16, 1], P('gy', 'gx'), may hold values from 0 to 15; in each aligned block of 16 rows (0 to 15, 16 to 31, ..., all dimensions but the last counted through in order) at most 2 rows name the same one
- w_conv: bfloat16 [9, 256, 256], replicated, may hold values from -0.125 to 0.125
- w_stride: bfloat16 [4, 256, 256], replicated, may hold values from -0.1875 to 0.1875
- w_query: float32 [256, 256], replicated, may hold values from -0.375 to 0.375
- w_key: float32 [256, 256], replicated, may hold values from -0.375 to 0.375
- w_value: float32 [256, 256], replicated, may hold values from -0.375 to 0.375
- cotangent: float32 [256], replicated, may hold values from -6 to 6
Outputs:
- embedding: float32 [256], replicated
- input_grad: bfloat16 [256, 2048, 256], P('gy', 'gx')
- conv_grad: float32 [9, 256, 256], replicated
Inputs may be any that keep to these rules, and one draw needn't show every extreme that they name: `owner_map`: among the tiles of one device, no owner index is named more than 2 times.
All inputs are finite; a program needn't handle non-finite values. No bound on the sum of `tissue` on one device may be relied on, other than what follows from the above.
Results may differ from a plain program's by a relative error of at most 0.017.
Values may be sent and summed in bfloat16 or wider, within the bound.
A program may use at most 128 MiB of HBM per device.

v0:
```python
from functools import partial
import math
import jax
import jax.numpy as jnp
from jax import lax
from jax.sharding import PartitionSpec as P

HEADS = 4
CAP = 2
attention_bias = -1.0
loss_scale = 512.0


def extended(block, sides, width):
    for axis, dim in sides:
        count = lax.axis_size(axis)
        forward = [(i, i + 1) for i in range(count - 1)]
        backward = [(target, source) for source, target in forward]
        low = lax.ppermute(
            lax.slice_in_dim(block, block.shape[dim] - width, None, axis=dim), axis, forward
        )
        high = lax.ppermute(lax.slice_in_dim(block, 0, width, axis=dim), axis, backward)
        block = jnp.concatenate([low, block, high], axis=dim)
    return block


def forward_taps(padded, weight, pix_rows, pix_cols):
    channels = padded.shape[2]
    running = jnp.zeros((pix_rows * pix_cols, weight.shape[2]), jnp.float32)
    for tap_index in range(9):
        row_off, col_off = (tap_index // 3, tap_index % 3)
        window = padded[row_off : row_off + pix_rows, col_off : col_off + pix_cols].reshape(
            pix_rows * pix_cols, channels
        )
        running = running + jnp.dot(window, weight[tap_index], preferred_element_type=jnp.float32)
    return running.reshape(pix_rows, pix_cols, weight.shape[2])


def backward_taps(padded, weight, pix_rows, pix_cols):
    channels = padded.shape[2]
    running = jnp.zeros((pix_rows * pix_cols, weight.shape[1]), jnp.float32)
    for tap_index in range(9):
        row_off, col_off = (tap_index // 3, tap_index % 3)
        window = padded[
            2 - row_off : 2 - row_off + pix_rows, 2 - col_off : 2 - col_off + pix_cols
        ].reshape(pix_rows * pix_cols, channels)
        running = running + lax.dot_general(
            window, weight[tap_index], (((1,), (1,)), ((), ())), preferred_element_type=jnp.float32
        )
    return running.reshape(pix_rows, pix_cols, weight.shape[1])


def weight_taps(padded, upstream, pix_rows, pix_cols):
    channels = padded.shape[2]
    flat_up = upstream.reshape(pix_rows * pix_cols, upstream.shape[2])
    pieces = []
    for tap_index in range(9):
        row_off, col_off = (tap_index // 3, tap_index % 3)
        window = padded[row_off : row_off + pix_rows, col_off : col_off + pix_cols].reshape(
            pix_rows * pix_cols, channels
        )
        pieces.append(
            lax.dot_general(
                window, flat_up, (((0,), (0,)), ((), ())), preferred_element_type=jnp.float32
            )
        )
    return jnp.stack(pieces)


def strided_forward(field, weight):
    pix_rows, pix_cols, channels = field.shape
    running = jnp.zeros((pix_rows // 2 * (pix_cols // 2), weight.shape[2]), jnp.float32)
    for tap_index in range(4):
        row_off, col_off = (tap_index // 2, tap_index % 2)
        window = field[row_off::2, col_off::2].reshape(-1, channels)
        running = running + jnp.dot(window, weight[tap_index], preferred_element_type=jnp.float32)
    return running.reshape(pix_rows // 2, pix_cols // 2, weight.shape[2])


def strided_backward(upstream, weight):
    half_rows, half_cols, channels = upstream.shape
    flat_up = upstream.reshape(half_rows * half_cols, channels)
    tap_parts = []
    for tap_index in range(4):
        tap_parts.append(
            lax.dot_general(
                flat_up,
                weight[tap_index],
                (((1,), (1,)), ((), ())),
                preferred_element_type=jnp.float32,
            ).reshape(half_rows, half_cols, -1)
        )
    upper_rows = jnp.stack([tap_parts[0], tap_parts[1]], axis=2)
    bottom = jnp.stack([tap_parts[2], tap_parts[3]], axis=2)
    stacked = jnp.stack([upper_rows, bottom], axis=1)
    return stacked.reshape(2 * half_rows, 2 * half_cols, -1)


def rms_normed(tokens_in):
    return tokens_in * lax.rsqrt(jnp.mean(tokens_in * tokens_in, axis=-1, keepdims=True) + 1e-05)


def silu_slope(values):
    gate_sig = jax.nn.sigmoid(values)
    return gate_sig * (1.0 + values * (1.0 - gate_sig))


def attend(
    query_tokens,
    query_flags,
    query_groups,
    key_tokens,
    key_flags,
    key_groups,
    w_query,
    w_key,
    w_value,
    head_count,
):
    highest = lax.Precision.HIGHEST
    query_count = query_tokens.shape[0]
    key_count = key_tokens.shape[0]
    query_rows = jnp.dot(query_tokens, w_query, precision=highest).reshape(
        query_count, head_count, -1
    )
    key_rows = jnp.dot(key_tokens, w_key, precision=highest).reshape(key_count, head_count, -1)
    value_rows = jnp.dot(key_tokens, w_value, precision=highest).reshape(key_count, head_count, -1)
    scores = jnp.einsum("qhd,khd->hqk", query_rows, key_rows, precision=highest) / math.sqrt(
        query_rows.shape[2]
    )
    allowed = (query_groups[:, None] == key_groups[None, :]).astype(jnp.float32) * key_flags[
        None, :
    ]
    weights = jax.nn.sigmoid(scores + attention_bias) * allowed[None]
    mixed_rows = jnp.einsum("hqk,khd->qhd", weights, value_rows, precision=highest).reshape(
        query_count, -1
    )
    return jnp.dot(query_flags, mixed_rows, precision=highest)


def self_attend(tokens_in, tile_flags, tile_groups, w_query, w_key, w_value, head_count):
    return attend(
        tokens_in,
        tile_flags,
        tile_groups,
        tokens_in,
        tile_flags,
        tile_groups,
        w_query,
        w_key,
        w_value,
        head_count,
    )


def per_device(features, tissue, owner_map, w_conv, w_stride, w_query, w_key, w_value, cotangent):
    pix_rows, pix_cols, channels = features.shape
    tile_rows, tile_cols = tissue.shape
    cell_side = pix_rows // (2 * tile_rows)
    gx_count = lax.axis_size("gx")
    tiles_all = tile_rows * tile_cols * lax.axis_size("gy") * gx_count
    norm_scale = 1.0 / math.sqrt(tiles_all)
    seed_grad = cotangent * (loss_scale * norm_scale)
    padded = extended(features, (("gy", 0), ("gx", 1)), 1)
    pre_act = forward_taps(padded, w_conv, pix_rows, pix_cols)
    pixel_mask = jnp.repeat(
        jnp.repeat(tissue.astype(jnp.float32), 2 * cell_side, axis=0), 2 * cell_side, axis=1
    )[:, :, None]
    summed = (features.astype(jnp.float32) + jax.nn.silu(pre_act) * pixel_mask).astype(jnp.bfloat16)
    reduced = strided_forward(summed, w_stride)
    pooled = (
        reduced.reshape(tile_rows, cell_side, tile_cols, cell_side, channels)
        .mean(axis=(1, 3))
        .reshape(-1, channels)
    )
    normed = rms_normed(pooled).astype(jnp.bfloat16)
    tile_flags = tissue.reshape(-1).astype(jnp.float32)
    owners = owner_map.reshape(-1)
    slot_count = gx_count * CAP
    choose = (owners[:, None] == jnp.arange(gx_count, dtype=jnp.int32)[None, :]).astype(jnp.int32)
    earlier = jnp.cumsum(choose, axis=0) - choose
    rank_in = jnp.sum(earlier * choose, axis=1)
    slot_of = owners * CAP + rank_in
    slot_place = (jnp.arange(slot_count, dtype=jnp.int32)[:, None] == slot_of[None, :]).astype(
        jnp.bfloat16
    )
    sent_tokens = (
        jnp.dot(slot_place, normed, preferred_element_type=jnp.float32)
        .astype(jnp.bfloat16)
        .reshape(gx_count, CAP, channels)
    )
    sent_flags = (
        jnp.dot(slot_place, tile_flags.astype(jnp.bfloat16), preferred_element_type=jnp.float32)
        .astype(jnp.bfloat16)
        .reshape(gx_count, CAP)
    )
    got_tokens, got_flags = (
        lax.all_to_all(sent_tokens, "gx", split_axis=0, concat_axis=0, tiled=True),
        lax.all_to_all(sent_flags, "gx", split_axis=0, concat_axis=0, tiled=True),
    )
    group_tokens = got_tokens.reshape(slot_count, channels).astype(jnp.float32)
    group_flags = got_flags.reshape(slot_count).astype(jnp.float32)
    group_ids = jnp.zeros((slot_count,), jnp.int32)
    group_fn = partial(
        self_attend,
        tile_flags=group_flags,
        tile_groups=group_ids,
        w_query=w_query,
        w_key=w_key,
        w_value=w_value,
        head_count=HEADS,
    )
    partial_sum, pull_group = jax.vjp(group_fn, group_tokens)
    slot_grads = pull_group(seed_grad)[0].astype(jnp.bfloat16).reshape(gx_count, CAP, channels)
    returned = lax.all_to_all(slot_grads, "gx", split_axis=0, concat_axis=0, tiled=True)
    token_grad = lax.dot_general(
        slot_place,
        returned.reshape(slot_count, channels),
        (((0,), (0,)), ((), ())),
        preferred_element_type=jnp.float32,
    )
    embedding = lax.psum(partial_sum, ("gy", "gx")) * norm_scale
    pooled_grad = jax.vjp(rms_normed, pooled)[1](token_grad)[0]
    cell_grad = (
        (pooled_grad / (cell_side * cell_side))
        .astype(jnp.bfloat16)
        .reshape(tile_rows, 1, tile_cols, 1, channels)
    )
    cell_grad = jnp.broadcast_to(
        cell_grad, (tile_rows, cell_side, tile_cols, cell_side, channels)
    ).reshape(pix_rows // 2, pix_cols // 2, channels)
    sum_grad = strided_backward(cell_grad, w_stride)
    pre_grad = (sum_grad * pixel_mask * silu_slope(pre_act)).astype(jnp.bfloat16)
    local_grads = weight_taps(padded, pre_grad, pix_rows, pix_cols)
    grad_pad = extended(pre_grad, (("gy", 0), ("gx", 1)), 1)
    input_grad = (sum_grad + backward_taps(grad_pad, w_conv, pix_rows, pix_cols)).astype(
        jnp.bfloat16
    )
    conv_grad = lax.psum(local_grads, ("gy", "gx"))
    conv_grad = conv_grad / loss_scale
    return (embedding, input_grad, conv_grad)


def solution(mesh):
    in_specs = (
        P("gy", "gx", None),
        P("gy", "gx"),
        P("gy", "gx", None, None),
        P(),
        P(),
        P(),
        P(),
        P(),
        P(),
    )
    out_specs = (P(), P("gy", "gx", None), P())
    return jax.shard_map(
        per_device, mesh=mesh, in_specs=in_specs, out_specs=out_specs, check_vma=False
    )
```

profile of v0, /device:TPU:1, one launch (start us, length us, event | category | flops | bytes accessed | tf_op | source)
XLA Modules:
  0.0 436.3 jit_solution(15999486301501065111)
XLA Ops:
  7.2 3.2 copy.54
  10.4 4.0 collective-permute-start
  14.5 1.3 collective-permute-start.1
  17.0 7.2 %all-to-all-start = ((bf16[16,1,2]{2,1,0:T(2,128)(2,1)}), bf16[16,1,2]{2,1,0:T(2,128)(2,1)}, u32[]{:S(2)}, u32[]{:S(2)}) async-start(bf16[16,1,2]{2,1,0:T(2,128)(2,1)} %all_to_all.16), calls=%async_computation | async-start | bytes 16384 | tf_op jit(solution)/shard_map/all_to_all | solution.py:199
  25.3 3.0 fusion.131
  28.3 2.2 copy.62
  30.5 2.2 copy.57
  32.7 3.5 collective-permute-start.2
  36.2 2.4 collective-permute-start.3
  38.7 2.3 pad_maximum_fusion.6
  41.0 4.1 copy.69
  45.0 4.1 copy.61
  49.1 1.9 copy.63
  51.0 1.9 copy.58
  52.9 7.1 %pad_maximum_fusion = (bf16[34,129,256]{1,2,0:T(8,128)(2,1)S(1)}, bf16[34,129,256]{1,2,0:T(8,128)(2,1)}) fusion(bf16[34,1,256]{1,2,0:T(8,128)(2,1)} %copy.63, bf16[1,128,256]{1,2,0:T(8,128)(2,1)S(1)} %collective-permute-done.1, bf16[32,128,256]{1,2,0:T(8,128)(2,1)S(1)} %copy.54, bf16[1,128,256]{1,2,0:T(8,128)(2,1)S(1)} %collective-permute-done, ...), kind=kLoop, calls=%fused_computation.17 | loop fusion | flops 17965056 | bytes 6754304 | tf_op jit(solution)/shard_map/concatenate | solution.py:23
  60.0 3.6 fusion.127
  63.6 4.1 copy.70
  67.7 4.1 copy.66
  71.8 2.9 copy.64
  74.7 5.8 %fusion.128 = (bf16[32,128,256]{1,2,0:T(8,128)(2,1)}, bf16[32,128,256]{1,2,0:T(8,128)(2,1)S(1)}, bf16[32,128,256]{1,2,0:T(8,128)(2,1)}) fusion(bf16[34,129,256]{1,2,0:T(8,128)(2,1)} %get-tuple-element.20), kind=kLoop, calls=%fused_computation.195 | loop fusion | bytes 12582912 | tf_op jit(solution)/shard_map/slice | solution.py:32
  80.4 4.1 copy.67
  84.5 2.9 copy.65
  87.4 3.4 copy.59
  94.7 0.9 copy-done.14
  96.3 0.9 copy-done.6
  104.2 2.1 copy-done.1
  106.3 1.7 add_convert_fusion.1
  108.0 5.3 %slice.187 = bf16[16,64,256]{2,1,0:T(8,128)(2,1)} slice(bf16[32,128,256]{2,1,0:T(8,128)(2,1)S(1)} %add_convert_fusion.1), slice={[1:32:2], [1:128:2], [0:256:1]} | slice | bytes 1048576 | tf_op jit(solution)/shard_map/slice | solution.py:75
  113.3 5.3 %slice.185 = bf16[16,64,256]{2,1,0:T(8,128)(2,1)} slice(bf16[32,128,256]{2,1,0:T(8,128)(2,1)S(1)} %add_convert_fusion.1), slice={[1:32:2], [0:128:2], [0:256:1]} | slice | bytes 1048576 | tf_op jit(solution)/shard_map/slice | solution.py:75
  118.5 5.3 %slice.183 = bf16[16,64,256]{2,1,0:T(8,128)(2,1)} slice(bf16[32,128,256]{2,1,0:T(8,128)(2,1)S(1)} %add_convert_fusion.1), slice={[0:32:2], [1:128:2], [0:256:1]} | slice | bytes 1048576 | tf_op jit(solution)/shard_map/slice | solution.py:75
  123.8 5.3 %slice.181 = bf16[16,64,256]{2,1,0:T(8,128)(2,1)} slice(bf16[32,128,256]{2,1,0:T(8,128)(2,1)S(1)} %add_convert_fusion.1), slice={[0:32:2], [0:128:2], [0:256:1]} | slice | bytes 1048576 | tf_op jit(solution)/shard_map/slice | solution.py:75
  129.1 1.4 fusion.46
  130.6 1.4 convolution_add_fusion.17
  134.4 5.8 %all-to-all-start.1 = ((bf16[16,2,256]{2,1,0:T(2,128)(2,1)}), bf16[16,2,256]{2,1,0:T(2,128)(2,1)S(1)}, u32[]{:S(2)}, u32[]{:S(2)}) async-start(bf16[16,2,256]{2,1,0:T(2,128)(2,1)} %reshape.228), calls=%async_computation.1 | async-start | bytes 32768 | tf_op jit(solution)/shard_map/all_to_all | solution.py:198
  143.9 2.1 all-to-all-done.1
  149.3 68.0 %psum.14 = f32[256]{0:T(256)S(1)} all-reduce(f32[256]{0:T(256)S(1)} %bitcast.295), channel_id=1, replica_groups=mesh['gy'=8,'gx'=16] {'gy','gx'}, use_global_device_ids=true, to_apply=%region_4.5 | all-reduce | flops 256 | bytes 2048 | tf_op jit(solution)/shard_map/psum | solution.py:222
  218.9 4.0 all-to-all-start.2
  223.5 5.2 %all-to-all-done.2 = bf16[16,2,256]{2,1,0:T(2,128)(2,1)S(1)} async-done(((bf16[16,2,256]{2,1,0:T(2,128)(2,1)}), bf16[16,2,256]{2,1,0:T(2,128)(2,1)S(1)}, u32[]{:S(2)}, u32[]{:S(2)}) %all-to-all-start.2) | async-done | bytes 16416 | tf_op jit(solution)/shard_map/all_to_all | solution.py:215
  231.3 5.2 %copy.82 = f32[16,2,64,2,256]{4,3,2,1,0:T(2,128)} copy(f32[16,2,64,2,256]{4,2,0,3,1:T(8,128)S(1)} %pad_maximum_fusion.1) | data formatting | bytes 8388608 | tf_op jit(solution)/shard_map/stack | solution.py:95
  236.5 6.2 %reshape.236 = f32[32,128,256]{2,1,0:T(8,128)} reshape(f32[16,2,64,2,256]{4,3,2,1,0:T(2,128)} %copy.82) | data formatting | bytes 8388608 | tf_op jit(solution)/shard_map/reshape | solution.py:96
  242.7 4.3 multiply_convert_fusion.1
  247.1 3.2 fusion.29
  250.3 2.1 collective-permute-start.4
  252.4 1.4 collective-permute-start.5
  253.8 1.4 fusion.20
  255.3 1.7 fusion.28
  257.0 1.4 fusion.27
  258.6 1.7 fusion.26
  260.2 1.7 fusion.25
  262.0 1.4 fusion.24
  263.4 1.4 fusion.14
  264.8 1.7 fusion.23
  266.6 6.1 %reshape.241 = f32[4096,256]{1,0:T(8,128)} reshape(f32[16,2,64,2,256]{4,3,2,1,0:T(2,128)} %copy.82) | data formatting | bytes 8388608 | tf_op jit(solution)/shard_map/reshape | solution.py:96
  272.7 2.6 collective-permute-start.6
  275.3 3.0 collective-permute-start.7
  279.4 1.5 pad_maximum_fusion.2
  280.9 1.6 fusion.129
  285.5 1.3 copy-done.2
  286.8 1.3 copy-done.16
  288.1 2.0 convolution_add_fusion.3
  293.3 1.4 copy-done
  294.7 2.0 add_convert_fusion
  296.7 129.2 %all-reduce.2.cloned.1.call-done = f32[9,256,256]{2,1,0:T(8,128)} async-done(((f32[9,256,256]{2,1,0:T(8,128)}), f32[9,256,256]{2,1,0:T(8,128)}) %all-reduce.2.cloned.1.call-update) | async-done | bytes 2359312 | tf_op jit(solution)/shard_map/psum | solution.py:239
  425.9 3.3 broadcast_multiply_fusion
  (173 shorter events, 35.2 us)
Async XLA Ops:
  7.2 8.6 %copy-start.31 = (s32[2,8]{1,0:T(2,128)S(1)}, s32[2,8]{1,0:T(2,128)}, u32[]{:S(2)}) copy-start(s32[2,8]{1,0:T(2,128)} %param.10) | copy-start | bytes 196
  7.2 8.7 %copy-start.30 = (s32[1,1,16,1]{2,3,1,0:T(1,128)S(1)}, s32[1,1,16,1]{2,3,1,0:T(1,128)}, u32[]{:S(2)}) copy-start(s32[1,1,16,1]{2,3,1,0:T(1,128)} %param.11) | copy-start | bytes 196
  10.4 42.5 %copy-start.3 = (bf16[32,128,256]{1,2,0:T(8,128)(2,1)}, bf16[32,128,256]{1,2,0:T(8,128)(2,1)S(1)}, u32[]{:S(2)}) copy-start(bf16[32,128,256]{1,2,0:T(8,128)(2,1)S(1)} %copy.54) | copy-start | bytes 6291460
  10.4 14.5 %collective-permute-start = (bf16[1,128,256]{1,2,0:T(8,128)(2,1)S(1)}, bf16[1,128,256]{1,2,0:T(8,128)(2,1)S(1)}, u32[]{:S(2)}, u32[]{:S(2)}) collective-permute-start(bf16[1,128,256]{1,2,0:T(8,128)(2,1)S(1)} %get-tuple-element.29), channel_id=1, source_target_pairs={{0,16},{16,32},{32,48},{48,64},{64,80},{80,96},{96,112},{1,17},{17... | collective-permute-start | bytes 196616 | tf_op jit(solution)/shard_map/ppermute | solution.py:19
  14.5 10.5 %collective-permute-start.1 = (bf16[1,128,256]{1,2,0:T(8,128)(2,1)S(1)}, bf16[1,128,256]{1,2,0:T(8,128)(2,1)S(1)}, u32[]{:S(2)}, u32[]{:S(2)}) collective-permute-start(bf16[1,128,256]{1,2,0:T(8,128)(2,1)S(1)} %get-tuple-element.30), channel_id=1, source_target_pairs={{16,0},{32,16},{48,32},{64,48},{80,64},{96,80},{112,96},{17,1},{33... | collective-permute-start | bytes 196616 | tf_op jit(solution)/shard_map/ppermute | solution.py:22
  16.2 8.1 %copy-start.32 = (s32[16]{0:T(128)}, s32[16]{0:T(128)S(1)}, u32[]{:S(2)}) copy-start(s32[16]{0:T(128)S(1)} %multiply_add_fusion.1) | copy-start | bytes 196
  17.0 117.4 %all-to-all-start = ((bf16[16,1,2]{2,1,0:T(2,128)(2,1)}), bf16[16,1,2]{2,1,0:T(2,128)(2,1)}, u32[]{:S(2)}, u32[]{:S(2)}) async-start(bf16[16,1,2]{2,1,0:T(2,128)(2,1)} %all_to_all.16), calls=%async_computation | async-start | bytes 16384 | tf_op jit(solution)/shard_map/all_to_all | solution.py:199
  24.3 0.6 copy-start.28
  25.0 27.9 %copy-start.26 = (bf16[1,128,256]{1,2,0:T(8,128)(2,1)}, bf16[1,128,256]{1,2,0:T(8,128)(2,1)S(1)}, u32[]{:S(2)}) copy-start(bf16[1,128,256]{1,2,0:T(8,128)(2,1)S(1)} %collective-permute-done) | copy-start | bytes 196612
  25.0 27.9 %copy-start.24 = (bf16[1,128,256]{1,2,0:T(8,128)(2,1)}, bf16[1,128,256]{1,2,0:T(8,128)(2,1)S(1)}, u32[]{:S(2)}) copy-start(bf16[1,128,256]{1,2,0:T(8,128)(2,1)S(1)} %collective-permute-done.1) | copy-start | bytes 196612
  32.7 18.3 %collective-permute-start.2 = (bf16[34,1,256]{2,0,1:T(8,128)(2,1)S(1)}, bf16[34,1,256]{2,0,1:T(8,128)(2,1)S(1)}, u32[]{:S(2)}, u32[]{:S(2)}) collective-permute-start(bf16[34,1,256]{2,0,1:T(8,128)(2,1)S(1)} %copy.57), channel_id=1, source_target_pairs={{0,1},{1,2},{2,3},{3,4},{4,5},{5,6},{6,7},{7,8},{8,9},{9,10},{10,1... | collective-permute-start | bytes 52232 | tf_op jit(solution)/shard_map/ppermute | solution.py:19
  36.2 12.9 %collective-permute-start.3 = (bf16[34,1,256]{2,0,1:T(8,128)(2,1)S(1)}, bf16[34,1,256]{2,0,1:T(8,128)(2,1)S(1)}, u32[]{:S(2)}, u32[]{:S(2)}) collective-permute-start(bf16[34,1,256]{2,0,1:T(8,128)(2,1)S(1)} %copy.62), channel_id=1, source_target_pairs={{1,0},{2,1},{3,2},{4,3},{5,4},{6,5},{7,6},{8,7},{9,8},{10,9},{11,1... | collective-permute-start | bytes 52232 | tf_op jit(solution)/shard_map/ppermute | solution.py:22
  60.0 3.6 copy-start.5
  87.4 3.4 copy-start.15
  90.8 1.6 copy-start.9
  92.4 1.6 copy-start.13
  94.0 1.6 copy-start.14
  95.5 1.6 copy-start.6
  97.1 1.6 copy-start.11
  98.7 1.6 copy-start.12
  100.3 1.6 copy-start.8
  101.9 1.6 copy-start.10
  104.2 2.1 copy-start.1
  129.1 2.9 copy-start.18
  129.1 2.9 copy-start.19
  130.6 1.8 copy-start.17
  132.3 10.2 %copy-start.23 = (f32[256,256]{1,0:T(8,128)S(1)}, f32[256,256]{1,0:T(8,128)}, u32[]{:S(2)}) copy-start(f32[256,256]{1,0:T(8,128)} %param.14) | copy-start | bytes 786436
  132.4 10.3 %copy-start.22 = (f32[256,256]{1,0:T(8,128)S(1)}, f32[256,256]{1,0:T(8,128)}, u32[]{:S(2)}) copy-start(f32[256,256]{1,0:T(8,128)} %param.15) | copy-start | bytes 786436
  132.4 10.4 %copy-start.21 = (f32[256,256]{1,0:T(8,128)S(1)}, f32[256,256]{1,0:T(8,128)}, u32[]{:S(2)}) copy-start(f32[256,256]{1,0:T(8,128)} %param.16) | copy-start | bytes 786436
  134.4 11.6 %all-to-all-start.1 = ((bf16[16,2,256]{2,1,0:T(2,128)(2,1)}), bf16[16,2,256]{2,1,0:T(2,128)(2,1)S(1)}, u32[]{:S(2)}, u32[]{:S(2)}) async-start(bf16[16,2,256]{2,1,0:T(2,128)(2,1)} %reshape.228), calls=%async_computation.1 | async-start | bytes 32768 | tf_op jit(solution)/shard_map/all_to_all | solution.py:198
  142.9 85.8 %copy-start.33 = (s32[16]{0:T(128)S(1)}, s32[16]{0:T(128)}, u32[]{:S(2)}) copy-start(s32[16]{0:T(128)} %copy-done.32) | copy-start | bytes 196
  146.6 82.5 %copy-start.20 = (bf16[4,256,256]{2,1,0:T(8,128)(2,1)S(1)}, bf16[4,256,256]{2,1,0:T(8,128)(2,1)}, u32[]{:S(2)}) copy-start(bf16[4,256,256]{2,1,0:T(8,128)(2,1)} %param.13) | copy-start | bytes 1572868
  218.9 9.8 %all-to-all-start.2 = ((bf16[16,2,256]{2,1,0:T(2,128)(2,1)}), bf16[16,2,256]{2,1,0:T(2,128)(2,1)S(1)}, u32[]{:S(2)}, u32[]{:S(2)}) async-start(bf16[16,2,256]{2,1,0:T(2,128)(2,1)} %reshape.234), calls=%async_computation.2 | async-start | bytes 32768 | tf_op jit(solution)/shard_map/all_to_all | solution.py:215
  222.9 203.1 %all-reduce.2.cloned.1.call-start = ((), (), s32[]{:S(2)}) async-start(), calls=%async_computation.3 | async-start | bytes 4718592 | tf_op jit(solution)/shard_map/psum | solution.py:239
  242.7 11.1 %copy-start.27 = (bf16[1,128,256]{1,2,0:T(8,128)(2,1)S(1)}, bf16[1,128,256]{1,2,0:T(8,128)(2,1)}, u32[]{:S(2)}) copy-start(bf16[1,128,256]{1,2,0:T(8,128)(2,1)} %copy-done.26) | copy-start | bytes 196612
  242.7 12.5 %slice-start = ((s8[4456448]{0:T(1024)(128)(4,1)}), s8[262144]{0:T(1024)(128)(4,1)S(1)}, s32[]{:S(2)}) async-start(s8[4456448]{0:T(1024)(128)(4,1)} %bitcast.258), calls=%async_computation.4 | async-start | bytes 524288
  247.1 6.7 %copy-start.4 = (bf16[32,128,256]{1,2,0:T(8,128)(2,1)S(1)}, bf16[32,128,256]{1,2,0:T(8,128)(2,1)}, u32[]{:S(2)}) copy-start(bf16[32,128,256]{1,2,0:T(8,128)(2,1)} %copy-done.3) | copy-start | bytes 6291460
  247.1 8.2 %slice-start.1 = ((s8[4456448]{0:T(1024)(128)(4,1)}), s8[4194304]{0:T(1024)(128)(4,1)S(1)}, s32[]{:S(2)}) async-start(s8[4456448]{0:T(1024)(128)(4,1)} %bitcast.258), calls=%async_computation.5 | async-start | bytes 8388608
  247.1 9.9 %slice-start.2 = ((s8[4456448]{0:T(1024)(128)(4,1)}), s8[4194304]{0:T(1024)(128)(4,1)S(1)}, s32[]{:S(2)}) async-start(s8[4456448]{0:T(1024)(128)(4,1)} %bitcast.260), calls=%async_computation.6 | async-start | bytes 8388608
  250.3 22.4 %collective-permute-start.4 = (bf16[1,128,256]{2,1,0:T(8,128)(2,1)S(1)}, bf16[1,128,256]{2,1,0:T(8,128)(2,1)S(1)}, u32[]{:S(2)}, u32[]{:S(2)}) collective-permute-start(bf16[1,128,256]{2,1,0:T(8,128)(2,1)S(1)} %get-tuple-element.25), channel_id=1, source_target_pairs={{0,16},{16,32},{32,48},{48,64},{64,80},{80,96},{96,112},{1,17},{17... | collective-permute-start | bytes 196616 | tf_op jit(solution)/shard_map/ppermute | solution.py:19
  252.4 4.6 %slice-start.3 = ((s8[4456448]{0:T(1024)(128)(4,1)}), s8[262144]{0:T(1024)(128)(4,1)S(1)}, s32[]{:S(2)}) async-start(s8[4456448]{0:T(1024)(128)(4,1)} %bitcast.260), calls=%async_computation.7 | async-start | bytes 524288
  252.4 20.3 %collective-permute-start.5 = (bf16[1,128,256]{2,1,0:T(8,128)(2,1)S(1)}, bf16[1,128,256]{2,1,0:T(8,128)(2,1)S(1)}, u32[]{:S(2)}, u32[]{:S(2)}) collective-permute-start(bf16[1,128,256]{2,1,0:T(8,128)(2,1)S(1)} %get-tuple-element.26), channel_id=1, source_target_pairs={{16,0},{32,16},{48,32},{64,48},{80,64},{96,80},{112,96},{17,1},{33... | collective-permute-start | bytes 196616 | tf_op jit(solution)/shard_map/ppermute | solution.py:22
  257.0 1.6 copy-start.7
  262.0 1.4 copy-start.25
  272.7 6.6 %collective-permute-start.6 = (bf16[34,1,256]{2,1,0:T(2,128)(2,1)S(1)}, bf16[34,1,256]{2,1,0:T(2,128)(2,1)S(1)}, u32[]{:S(2)}, u32[]{:S(2)}) collective-permute-start(bf16[34,1,256]{2,1,0:T(2,128)(2,1)S(1)} %get-tuple-element.17), channel_id=1, source_target_pairs={{1,0},{2,1},{3,2},{4,3},{5,4},{6,5},{7,6},{8,7},{9,8},{10,9},{11,1... | collective-permute-start | bytes 52232 | tf_op jit(solution)/shard_map/ppermute | solution.py:22
  275.3 4.0 collective-permute-start.7
  284.6 2.2 copy-start.2
  284.6 3.5 copy-start.16
  284.6 3.5 copy-start.29
  292.5 2.2 copy-start
Sparse Core Ops, SparseCore 0:
  272.8 153.1 all-reduce.1
where the time goes:
time: 441 us; the launch traced here: 436 us
  waiting for transfers between devices  137 us (31%)
  local copies, waits for them, and re-layouts  113 us (26%)
  blocking collectives  68 us (15%)
  matrix products  39.9 us (9%)
  starting transfers between devices  37.4 us (8%)
  other arithmetic  26.1 us (6%)
  between operations  15.2 us (3%)
    psum x1, waiting for transfers between devices, per_device(): conv_grad = lax.psum(local_grads, ('gy', 'gx'))  129 us
    psum x1, blocking collectives, per_device(): embedding = lax.psum(partial_sum, ('gy', 'gx')) * norm_scale  68 us
    slice x10, local copies, waits for them, and re-layouts, forward_taps(): padded[row_off:row_off + pix_rows, col_off:col_off + pix_cols]  38.9 us
    slice x4, local copies, waits for them, and re-layouts, strided_forward(): window = field[row_off::2, col_off::2].reshape(-1, channels)  21.1 us
    unnamed x81, local copies, waits for them, and re-layouts  17.7 us
    dot_general x9, matrix products, weight_taps(): lax.dot_general(window, flat_up, (((0,), (0,)), ((), ())), preferred_elem...  15.7 us
    ppermute x4, starting transfers between devices, extended(): lax.ppermute(lax.slice_in_dim(block, block.shape[dim] - width, None, axis...  12.6 us
    reshape x2, local copies, waits for them, and re-layouts, strided_backward(): return stacked.reshape(2 * half_rows, 2 * half_cols, -1)  12.3 us
  transfers between devices with their start and end apart: 12, of which 3 were waited for; matrix products, arithmetic and copies ran while one was open for 30% of the time, Pallas kernels for 0%

commit v1 on v0

--- a/solution.py
+++ b/solution.py
@@ -219,7 +219,7 @@
         (((0,), (0,)), ((), ())),
         preferred_element_type=jnp.float32,
     )
-    embedding = lax.psum(partial_sum, ("gy", "gx")) * norm_scale
+    embedding = lax.psum(lax.psum(partial_sum, "gx"), "gy") * norm_scale
     pooled_grad = jax.vjp(rms_normed, pooled)[1](token_grad)[0]
     cell_grad = (
         (pooled_grad / (cell_side * cell_side))

time: 441 us -> 426 us (0.966)
  blocking collectives: 68 us -> 48.3 us
    psum x1 -> x2, blocking collectives: 68 us -> 48.3 us  [per_device(): embedding = lax.psum(lax.psum(partial_sum, 'gx'), 'gy') * norm_scale]
    all_to_all x1, starting transfers between devices: 3.96 us -> 9.06 us  [per_device(): lax.all_to_all(slot_grads, 'gx', split_axis=0, concat_axis=0, tiled=True)]
  transfers between devices with their start and end apart: 12 -> 12, of which waited for: 3 -> 3; matrix products, arithmetic and copies ran while one was open for 30% -> 31% of each run, Pallas kernels for 0% -> 0%
where the time goes in v1:
time: 426 us; the launch traced here: 421 us
  waiting for transfers between devices  137 us (32%)
  local copies, waits for them, and re-layouts  113 us (27%)
  blocking collectives  48.3 us (11%)
  starting transfers between devices  41.6 us (10%)
  matrix products  39.9 us (9%)
  other arithmetic  26.5 us (6%)
  between operations  15.1 us (4%)
    psum x1, waiting for transfers between devices, per_device(): conv_grad = lax.psum(local_grads, ('gy', 'gx'))  129 us
    psum x2, blocking collectives, per_device(): embedding = lax.psum(lax.psum(partial_sum, 'gx'), 'gy') * norm_scale  48.3 us
    slice x10, local copies, waits for them, and re-layouts, forward_taps(): padded[row_off:row_off + pix_rows, col_off:col_off + pix_cols]  38.9 us
    slice x4, local copies, waits for them, and re-layouts, strided_forward(): window = field[row_off::2, col_off::2].reshape(-1, channels)  21.3 us
    unnamed x81, local copies, waits for them, and re-layouts  17.7 us
    dot_general x9, matrix products, weight_taps(): lax.dot_general(window, flat_up, (((0,), (0,)), ((), ())), preferred_elem...  15.7 us
    reshape x2, local copies, waits for them, and re-layouts, strided_backward(): return stacked.reshape(2 * half_rows, 2 * half_cols, -1)  12.2 us
    ppermute x4, starting transfers between devices, extended(): lax.ppermute(lax.slice_in_dim(block, block.shape[dim] - width, None, axis...  12.2 us
  transfers between devices with their start and end apart: 12, of which 3 were waited for; matrix products, arithmetic and copies ran while one was open for 31% of the time, Pallas kernels for 0%

profile of v1, /device:TPU:1, one launch (start us, length us, event | category | flops | bytes accessed | tf_op | source)
XLA Modules:
  0.0 421.4 jit_solution(16157160374194179427)
XLA Ops:
  7.2 3.2 copy.54
  10.4 4.0 collective-permute-start
  14.5 1.3 collective-permute-start.1
  17.0 7.2 %all-to-all-start = ((bf16[16,1,2]{2,1,0:T(2,128)(2,1)}), bf16[16,1,2]{2,1,0:T(2,128)(2,1)}, u32[]{:S(2)}, u32[]{:S(2)}) async-start(bf16[16,1,2]{2,1,0:T(2,128)(2,1)} %all_to_all.16), calls=%async_computation | async-start | bytes 16384 | tf_op jit(solution)/shard_map/all_to_all | solution.py:199
  25.3 3.0 fusion.131
  28.3 2.2 copy.62
  30.5 2.2 copy.57
  32.7 3.5 collective-permute-start.2
  36.2 2.2 collective-permute-start.3
  38.5 2.3 pad_maximum_fusion.6
  40.7 4.1 copy.69
  44.8 4.1 copy.61
  48.9 1.9 copy.63
  50.8 1.9 copy.58
  52.7 7.2 %pad_maximum_fusion = (bf16[34,129,256]{1,2,0:T(8,128)(2,1)S(1)}, bf16[34,129,256]{1,2,0:T(8,128)(2,1)}) fusion(bf16[34,1,256]{1,2,0:T(8,128)(2,1)} %copy.63, bf16[1,128,256]{1,2,0:T(8,128)(2,1)S(1)} %collective-permute-done.1, bf16[32,128,256]{1,2,0:T(8,128)(2,1)S(1)} %copy.54, bf16[1,128,256]{1,2,0:T(8,128)(2,1)S(1)} %collective-permute-done, ...), kind=kLoop, calls=%fused_computation.17 | loop fusion | flops 17965056 | bytes 6754304 | tf_op jit(solution)/shard_map/concatenate | solution.py:23
  59.9 3.6 fusion.127
  63.5 4.1 copy.70
  67.6 4.1 copy.66
  71.7 2.9 copy.64
  74.6 5.8 %fusion.128 = (bf16[32,128,256]{1,2,0:T(8,128)(2,1)}, bf16[32,128,256]{1,2,0:T(8,128)(2,1)S(1)}, bf16[32,128,256]{1,2,0:T(8,128)(2,1)}) fusion(bf16[34,129,256]{1,2,0:T(8,128)(2,1)} %get-tuple-element.20), kind=kLoop, calls=%fused_computation.195 | loop fusion | bytes 12582912 | tf_op jit(solution)/shard_map/slice | solution.py:32
  80.3 4.1 copy.67
  84.4 2.9 copy.65
  87.3 3.4 copy.59
  99.4 0.9 copy-done.12
  104.1 2.1 copy-done.1
  106.2 2.0 add_convert_fusion.1
  108.3 5.4 %slice.187 = bf16[16,64,256]{2,1,0:T(8,128)(2,1)} slice(bf16[32,128,256]{2,1,0:T(8,128)(2,1)S(1)} %add_convert_fusion.1), slice={[1:32:2], [1:128:2], [0:256:1]} | slice | bytes 1048576 | tf_op jit(solution)/shard_map/slice | solution.py:75
  113.6 5.3 %slice.185 = bf16[16,64,256]{2,1,0:T(8,128)(2,1)} slice(bf16[32,128,256]{2,1,0:T(8,128)(2,1)S(1)} %add_convert_fusion.1), slice={[1:32:2], [0:128:2], [0:256:1]} | slice | bytes 1048576 | tf_op jit(solution)/shard_map/slice | solution.py:75
  118.9 5.3 %slice.183 = bf16[16,64,256]{2,1,0:T(8,128)(2,1)} slice(bf16[32,128,256]{2,1,0:T(8,128)(2,1)S(1)} %add_convert_fusion.1), slice={[0:32:2], [1:128:2], [0:256:1]} | slice | bytes 1048576 | tf_op jit(solution)/shard_map/slice | solution.py:75
  124.2 5.3 %slice.181 = bf16[16,64,256]{2,1,0:T(8,128)(2,1)} slice(bf16[32,128,256]{2,1,0:T(8,128)(2,1)S(1)} %add_convert_fusion.1), slice={[0:32:2], [0:128:2], [0:256:1]} | slice | bytes 1048576 | tf_op jit(solution)/shard_map/slice | solution.py:75
  129.5 1.4 fusion.46
  131.0 1.4 convolution_add_fusion.17
  134.8 5.8 %all-to-all-start.1 = ((bf16[16,2,256]{2,1,0:T(2,128)(2,1)}), bf16[16,2,256]{2,1,0:T(2,128)(2,1)S(1)}, u32[]{:S(2)}, u32[]{:S(2)}) async-start(bf16[16,2,256]{2,1,0:T(2,128)(2,1)} %reshape.228), calls=%async_computation.1 | async-start | bytes 32768 | tf_op jit(solution)/shard_map/all_to_all | solution.py:198
  144.2 2.1 all-to-all-done.1
  149.6 26.9 %psum.21 = f32[256]{0:T(256)S(1)} all-reduce(f32[256]{0:T(256)S(1)} %bitcast.295), channel_id=1, replica_groups=mesh['gy'=8,'gx'=16] {'gx'}, use_global_device_ids=true, to_apply=%region_4.5 | all-reduce | flops 256 | bytes 2048 | tf_op jit(solution)/shard_map/psum | solution.py:222
  176.5 21.4 %psum.22 = f32[256]{0:T(256)S(1)} all-reduce(f32[256]{0:T(256)S(1)} %psum.21), channel_id=1, replica_groups=mesh['gy'=8,'gx'=16] {'gy'}, use_global_device_ids=true, to_apply=%region_5.6 | all-reduce | flops 256 | bytes 2048 | tf_op jit(solution)/shard_map/psum | solution.py:222
  199.6 9.1 %all-to-all-start.2 = ((bf16[16,2,256]{2,1,0:T(2,128)(2,1)}), bf16[16,2,256]{2,1,0:T(2,128)(2,1)S(1)}, u32[]{:S(2)}, u32[]{:S(2)}) async-start(bf16[16,2,256]{2,1,0:T(2,128)(2,1)} %reshape.234), calls=%async_computation.2 | async-start | bytes 32768 | tf_op jit(solution)/shard_map/all_to_all | solution.py:215
  209.3 5.2 %all-to-all-done.2 = bf16[16,2,256]{2,1,0:T(2,128)(2,1)S(1)} async-done(((bf16[16,2,256]{2,1,0:T(2,128)(2,1)}), bf16[16,2,256]{2,1,0:T(2,128)(2,1)S(1)}, u32[]{:S(2)}, u32[]{:S(2)}) %all-to-all-start.2) | async-done | bytes 16416 | tf_op jit(solution)/shard_map/all_to_all | solution.py:215
  217.1 5.2 %copy.82 = f32[16,2,64,2,256]{4,3,2,1,0:T(2,128)} copy(f32[16,2,64,2,256]{4,2,0,3,1:T(8,128)S(1)} %pad_maximum_fusion.1) | data formatting | bytes 8388608 | tf_op jit(solution)/shard_map/stack | solution.py:95
  222.4 6.2 %reshape.236 = f32[32,128,256]{2,1,0:T(8,128)} reshape(f32[16,2,64,2,256]{4,3,2,1,0:T(2,128)} %copy.82) | data formatting | bytes 8388608 | tf_op jit(solution)/shard_map/reshape | solution.py:96
  228.6 4.3 %multiply_convert_fusion.1 = bf16[32,128,256]{2,1,0:T(8,128)(2,1)S(1)} fusion(f32[32,128,256]{2,1,0:T(8,128)} %bitcast.257, f32[32,128,256]{2,1,0:T(8,128)} %reshape.236, f32[32,128]{1,0:T(8,128)S(1)} %copy.72), kind=kLoop, calls=%fused_computation.21 | loop fusion | flops 10485760 | bytes 10502144 | tf_op jit(solution)/shard_map/convert_element_type | solution.py:233
  232.9 3.2 fusion.29
  236.1 1.4 collective-permute-start.4
  237.5 1.4 collective-permute-start.5
  239.0 1.4 fusion.20
  240.4 1.7 fusion.28
  242.2 1.4 fusion.27
  243.7 1.7 fusion.26
  245.4 1.7 fusion.25
  247.1 1.4 fusion.24
  248.6 1.4 fusion.14
  250.0 1.7 fusion.23
  251.7 6.0 %reshape.241 = f32[4096,256]{1,0:T(8,128)} reshape(f32[16,2,64,2,256]{4,3,2,1,0:T(2,128)} %copy.82) | data formatting | bytes 8388608 | tf_op jit(solution)/shard_map/reshape | solution.py:96
  257.9 2.3 collective-permute-start.6
  260.2 3.3 collective-permute-start.7
  264.5 1.5 pad_maximum_fusion.2
  266.0 1.6 fusion.129
  270.6 1.3 copy-done.2
  271.9 1.3 copy-done.16
  273.2 2.0 convolution_add_fusion.3
  278.4 1.4 copy-done
  279.8 2.0 add_convert_fusion
  281.8 129.3 %all-reduce.2.cloned.1.call-done = f32[9,256,256]{2,1,0:T(8,128)} async-done(((f32[9,256,256]{2,1,0:T(8,128)}), f32[9,256,256]{2,1,0:T(8,128)}) %all-reduce.2.cloned.1.call-update) | async-done | bytes 2359312 | tf_op jit(solution)/shard_map/psum | solution.py:239
  411.1 3.3 broadcast_multiply_fusion
  (174 shorter events, 36.0 us)
Async XLA Ops:
  7.2 8.6 %copy-start.31 = (s32[2,8]{1,0:T(2,128)S(1)}, s32[2,8]{1,0:T(2,128)}, u32[]{:S(2)}) copy-start(s32[2,8]{1,0:T(2,128)} %param.10) | copy-start | bytes 196
  7.2 8.7 %copy-start.30 = (s32[1,1,16,1]{2,3,1,0:T(1,128)S(1)}, s32[1,1,16,1]{2,3,1,0:T(1,128)}, u32[]{:S(2)}) copy-start(s32[1,1,16,1]{2,3,1,0:T(1,128)} %param.11) | copy-start | bytes 196
  10.4 42.3 %copy-start.3 = (bf16[32,128,256]{1,2,0:T(8,128)(2,1)}, bf16[32,128,256]{1,2,0:T(8,128)(2,1)S(1)}, u32[]{:S(2)}) copy-start(bf16[32,128,256]{1,2,0:T(8,128)(2,1)S(1)} %copy.54) | copy-start | bytes 6291460
  10.4 14.6 %collective-permute-start = (bf16[1,128,256]{1,2,0:T(8,128)(2,1)S(1)}, bf16[1,128,256]{1,2,0:T(8,128)(2,1)S(1)}, u32[]{:S(2)}, u32[]{:S(2)}) collective-permute-start(bf16[1,128,256]{1,2,0:T(8,128)(2,1)S(1)} %get-tuple-element.29), channel_id=1, source_target_pairs={{0,16},{16,32},{32,48},{48,64},{64,80},{80,96},{96,112},{1,17},{17... | collective-permute-start | bytes 196616 | tf_op jit(solution)/shard_map/ppermute | solution.py:19
  14.5 10.5 %collective-permute-start.1 = (bf16[1,128,256]{1,2,0:T(8,128)(2,1)S(1)}, bf16[1,128,256]{1,2,0:T(8,128)(2,1)S(1)}, u32[]{:S(2)}, u32[]{:S(2)}) collective-permute-start(bf16[1,128,256]{1,2,0:T(8,128)(2,1)S(1)} %get-tuple-element.30), channel_id=1, source_target_pairs={{16,0},{32,16},{48,32},{64,48},{80,64},{96,80},{112,96},{17,1},{33... | collective-permute-start | bytes 196616 | tf_op jit(solution)/shard_map/ppermute | solution.py:22
  16.2 8.1 %copy-start.32 = (s32[16]{0:T(128)}, s32[16]{0:T(128)S(1)}, u32[]{:S(2)}) copy-start(s32[16]{0:T(128)S(1)} %multiply_add_fusion.1) | copy-start | bytes 196
  17.0 117.7 %all-to-all-start = ((bf16[16,1,2]{2,1,0:T(2,128)(2,1)}), bf16[16,1,2]{2,1,0:T(2,128)(2,1)}, u32[]{:S(2)}, u32[]{:S(2)}) async-start(bf16[16,1,2]{2,1,0:T(2,128)(2,1)} %all_to_all.16), calls=%async_computation | async-start | bytes 16384 | tf_op jit(solution)/shard_map/all_to_all | solution.py:199
  24.3 0.6 copy-start.28
  25.0 27.7 %copy-start.26 = (bf16[1,128,256]{1,2,0:T(8,128)(2,1)}, bf16[1,128,256]{1,2,0:T(8,128)(2,1)S(1)}, u32[]{:S(2)}) copy-start(bf16[1,128,256]{1,2,0:T(8,128)(2,1)S(1)} %collective-permute-done) | copy-start | bytes 196612
  25.0 27.7 %copy-start.24 = (bf16[1,128,256]{1,2,0:T(8,128)(2,1)}, bf16[1,128,256]{1,2,0:T(8,128)(2,1)S(1)}, u32[]{:S(2)}) copy-start(bf16[1,128,256]{1,2,0:T(8,128)(2,1)S(1)} %collective-permute-done.1) | copy-start | bytes 196612
  32.7 18.1 %collective-permute-start.2 = (bf16[34,1,256]{2,0,1:T(8,128)(2,1)S(1)}, bf16[34,1,256]{2,0,1:T(8,128)(2,1)S(1)}, u32[]{:S(2)}, u32[]{:S(2)}) collective-permute-start(bf16[34,1,256]{2,0,1:T(8,128)(2,1)S(1)} %copy.57), channel_id=1, source_target_pairs={{0,1},{1,2},{2,3},{3,4},{4,5},{5,6},{6,7},{7,8},{8,9},{9,10},{10,1... | collective-permute-start | bytes 52232 | tf_op jit(solution)/shard_map/ppermute | solution.py:19
  36.2 12.6 %collective-permute-start.3 = (bf16[34,1,256]{2,0,1:T(8,128)(2,1)S(1)}, bf16[34,1,256]{2,0,1:T(8,128)(2,1)S(1)}, u32[]{:S(2)}, u32[]{:S(2)}) collective-permute-start(bf16[34,1,256]{2,0,1:T(8,128)(2,1)S(1)} %copy.62), channel_id=1, source_target_pairs={{1,0},{2,1},{3,2},{4,3},{5,4},{6,5},{7,6},{8,7},{9,8},{10,9},{11,1... | collective-permute-start | bytes 52232 | tf_op jit(solution)/shard_map/ppermute | solution.py:22
  59.9 3.6 copy-start.5
  87.3 3.4 copy-start.15
  90.7 1.6 copy-start.9
  92.3 1.6 copy-start.13
  93.9 1.6 copy-start.14
  95.5 1.6 copy-start.6
  97.0 1.6 copy-start.11
  98.6 1.6 copy-start.12
  100.2 1.6 copy-start.8
  101.8 1.6 copy-start.10
  104.1 2.1 copy-start.1
  129.5 2.9 copy-start.18
  129.5 2.9 copy-start.19
  131.0 1.8 copy-start.17
  132.7 10.1 %copy-start.23 = (f32[256,256]{1,0:T(8,128)S(1)}, f32[256,256]{1,0:T(8,128)}, u32[]{:S(2)}) copy-start(f32[256,256]{1,0:T(8,128)} %param.14) | copy-start | bytes 786436
  132.8 10.2 %copy-start.22 = (f32[256,256]{1,0:T(8,128)S(1)}, f32[256,256]{1,0:T(8,128)}, u32[]{:S(2)}) copy-start(f32[256,256]{1,0:T(8,128)} %param.15) | copy-start | bytes 786436
  132.8 10.4 %copy-start.21 = (f32[256,256]{1,0:T(8,128)S(1)}, f32[256,256]{1,0:T(8,128)}, u32[]{:S(2)}) copy-start(f32[256,256]{1,0:T(8,128)} %param.16) | copy-start | bytes 786436
  134.8 11.6 %all-to-all-start.1 = ((bf16[16,2,256]{2,1,0:T(2,128)(2,1)}), bf16[16,2,256]{2,1,0:T(2,128)(2,1)S(1)}, u32[]{:S(2)}, u32[]{:S(2)}) async-start(bf16[16,2,256]{2,1,0:T(2,128)(2,1)} %reshape.228), calls=%async_computation.1 | async-start | bytes 32768 | tf_op jit(solution)/shard_map/all_to_all | solution.py:198
  143.3 71.2 %copy-start.33 = (s32[16]{0:T(128)S(1)}, s32[16]{0:T(128)}, u32[]{:S(2)}) copy-start(s32[16]{0:T(128)} %copy-done.32) | copy-start | bytes 196
  147.0 68.0 %copy-start.20 = (bf16[4,256,256]{2,1,0:T(8,128)(2,1)S(1)}, bf16[4,256,256]{2,1,0:T(8,128)(2,1)}, u32[]{:S(2)}) copy-start(bf16[4,256,256]{2,1,0:T(8,128)(2,1)} %param.13) | copy-start | bytes 1572868
  199.6 14.9 %all-to-all-start.2 = ((bf16[16,2,256]{2,1,0:T(2,128)(2,1)}), bf16[16,2,256]{2,1,0:T(2,128)(2,1)S(1)}, u32[]{:S(2)}, u32[]{:S(2)}) async-start(bf16[16,2,256]{2,1,0:T(2,128)(2,1)} %reshape.234), calls=%async_computation.2 | async-start | bytes 32768 | tf_op jit(solution)/shard_map/all_to_all | solution.py:215
  208.7 202.4 %all-reduce.2.cloned.1.call-start = ((), (), s32[]{:S(2)}) async-start(), calls=%async_computation.3 | async-start | bytes 4718592 | tf_op jit(solution)/shard_map/psum | solution.py:239
  228.6 10.4 %copy-start.27 = (bf16[1,128,256]{1,2,0:T(8,128)(2,1)S(1)}, bf16[1,128,256]{1,2,0:T(8,128)(2,1)}, u32[]{:S(2)}) copy-start(bf16[1,128,256]{1,2,0:T(8,128)(2,1)} %copy-done.26) | copy-start | bytes 196612
  228.6 11.8 %slice-start = ((s8[4456448]{0:T(1024)(128)(4,1)}), s8[262144]{0:T(1024)(128)(4,1)S(1)}, s32[]{:S(2)}) async-start(s8[4456448]{0:T(1024)(128)(4,1)} %bitcast.258), calls=%async_computation.4 | async-start | bytes 524288
  232.9 6.1 %copy-start.4 = (bf16[32,128,256]{1,2,0:T(8,128)(2,1)S(1)}, bf16[32,128,256]{1,2,0:T(8,128)(2,1)}, u32[]{:S(2)}) copy-start(bf16[32,128,256]{1,2,0:T(8,128)(2,1)} %copy-done.3) | copy-start | bytes 6291460
  232.9 7.5 %slice-start.1 = ((s8[4456448]{0:T(1024)(128)(4,1)}), s8[4194304]{0:T(1024)(128)(4,1)S(1)}, s32[]{:S(2)}) async-start(s8[4456448]{0:T(1024)(128)(4,1)} %bitcast.258), calls=%async_computation.5 | async-start | bytes 8388608
  232.9 9.2 %slice-start.2 = ((s8[4456448]{0:T(1024)(128)(4,1)}), s8[4194304]{0:T(1024)(128)(4,1)S(1)}, s32[]{:S(2)}) async-start(s8[4456448]{0:T(1024)(128)(4,1)} %bitcast.260), calls=%async_computation.6 | async-start | bytes 8388608
  236.1 21.7 %collective-permute-start.4 = (bf16[1,128,256]{2,1,0:T(8,128)(2,1)S(1)}, bf16[1,128,256]{2,1,0:T(8,128)(2,1)S(1)}, u32[]{:S(2)}, u32[]{:S(2)}) collective-permute-start(bf16[1,128,256]{2,1,0:T(8,128)(2,1)S(1)} %get-tuple-element.25), channel_id=1, source_target_pairs={{0,16},{16,32},{32,48},{48,64},{64,80},{80,96},{96,112},{1,17},{17... | collective-permute-start | bytes 196616 | tf_op jit(solution)/shard_map/ppermute | solution.py:19
  237.5 4.6 %slice-start.3 = ((s8[4456448]{0:T(1024)(128)(4,1)}), s8[262144]{0:T(1024)(128)(4,1)S(1)}, s32[]{:S(2)}) async-start(s8[4456448]{0:T(1024)(128)(4,1)} %bitcast.260), calls=%async_computation.7 | async-start | bytes 524288
  237.5 20.3 %collective-permute-start.5 = (bf16[1,128,256]{2,1,0:T(8,128)(2,1)S(1)}, bf16[1,128,256]{2,1,0:T(8,128)(2,1)S(1)}, u32[]{:S(2)}, u32[]{:S(2)}) collective-permute-start(bf16[1,128,256]{2,1,0:T(8,128)(2,1)S(1)} %get-tuple-element.26), channel_id=1, source_target_pairs={{16,0},{32,16},{48,32},{64,48},{80,64},{96,80},{112,96},{17,1},{33... | collective-permute-start | bytes 196616 | tf_op jit(solution)/shard_map/ppermute | solution.py:22
  242.1 1.6 copy-start.7
  247.1 1.4 copy-start.25
  257.9 6.6 %collective-permute-start.6 = (bf16[34,1,256]{2,1,0:T(2,128)(2,1)S(1)}, bf16[34,1,256]{2,1,0:T(2,128)(2,1)S(1)}, u32[]{:S(2)}, u32[]{:S(2)}) collective-permute-start(bf16[34,1,256]{2,1,0:T(2,128)(2,1)S(1)} %get-tuple-element.17), channel_id=1, source_target_pairs={{1,0},{2,1},{3,2},{4,3},{5,4},{6,5},{7,6},{8,7},{9,8},{10,9},{11,1... | collective-permute-start | bytes 52232 | tf_op jit(solution)/shard_map/ppermute | solution.py:22
  260.2 4.3 %collective-permute-start.7 = (bf16[34,1,256]{2,1,0:T(2,128)(2,1)S(1)}, bf16[34,1,256]{2,1,0:T(2,128)(2,1)S(1)}, u32[]{:S(2)}, u32[]{:S(2)}) collective-permute-start(bf16[34,1,256]{2,1,0:T(2,128)(2,1)S(1)} %get-tuple-element.18), channel_id=1, source_target_pairs={{0,1},{1,2},{2,3},{3,4},{4,5},{5,6},{6,7},{7,8},{8,9},{9,10},{10,1... | collective-permute-start | bytes 52232 | tf_op jit(solution)/shard_map/ppermute | solution.py:19
  269.7 2.2 copy-start.2
  269.7 3.5 copy-start.16
  269.7 3.5 copy-start.29
  277.5 2.2 copy-start
Sparse Core Ops, SparseCore 0:
  257.9 153.1 all-reduce.1
